TPU v7x, 32 devices: a whole 2x2x4 slice. The times are simulated.
32 devices in a mesh: pb: 4 (over y, core), kv: 8 (over z, x).
Axes of the slice: x: 2, y: 2, z: 4, core: 2. Of those that a mesh axis runs over, the one named last changes fastest.
Arguments:
- queries: bfloat16 [8192, 128], P(('pb', 'kv')), may hold values from -15 to 15
- query_tangent: bfloat16 [8192, 128], P(('pb', 'kv')), may hold values from -2 to 2
- keys: bfloat16 [8192, 128], P(('pb', 'kv')), may hold values from -8 to 8
- values: bfloat16 [8192, 128], P(('pb', 'kv')), may hold values from -6 to 6
- key_tangent: bfloat16 [8192, 128], P(('pb', 'kv')), may hold values from -2 to 2
- value_tangent: bfloat16 [8192, 128], P(('pb', 'kv')), may hold values from -6 to 6
- block_list: int32 [64, 8, 8], P('pb', 'kv'), may hold values from 0 to 63, as said below
- block_count: int32 [64, 8], P('pb', 'kv'), may hold values from 1 to 8, as said below
Outputs:
- attended: bfloat16 [8192, 128], P(('pb', 'kv'))
- attended_tangent: bfloat16 [8192, 128], P(('pb', 'kv'))
Inputs may be any that keep to these rules, and one draw needn't show every extreme that they name: `block_list`: entries for one query block and slab j are distinct key blocks g whose index g // (256 // 128) leaves remainder j when divided by 8; entries past block_count are valid but unused. `block_count`: the value 8 is reached in every key slab.
All inputs are finite; a program needn't handle non-finite values.
Results may differ from a plain program's by a relative error of at most 0.01.
Values may be sent and summed in bfloat16 or wider, within the bound.
A program may use at most 128 MiB of HBM per device.

v0:
```python
import math
import jax
import jax.numpy as jnp
from jax import lax
from jax.sharding import PartitionSpec as P

BLK = 128
LMAX = 8


def shards(
    queries, query_tangent, keys, values, key_tangent, value_tangent, block_list, block_count
):
    head_dim = queries.shape[1]
    shard_rows = keys.shape[0]
    shard_blocks = shard_rows // BLK
    slab_count = lax.axis_size("kv")
    score_scale = 1.0 / math.sqrt(head_dim)
    query_all, qtangent_all = (
        lax.all_gather(queries, "kv", axis=0, tiled=True),
        lax.all_gather(query_tangent, "kv", axis=0, tiled=True),
    )
    key_all, value_all, ktangent_all, vtangent_all = (
        lax.all_gather(keys, "pb", axis=0, tiled=True),
        lax.all_gather(values, "pb", axis=0, tiled=True),
        lax.all_gather(key_tangent, "pb", axis=0, tiled=True),
        lax.all_gather(value_tangent, "pb", axis=0, tiled=True),
    )
    key_blocks = key_all.reshape(-1, BLK, head_dim)
    value_blocks = value_all.reshape(-1, BLK, head_dim)
    keyt_blocks = ktangent_all.reshape(-1, BLK, head_dim)
    valuet_blocks = vtangent_all.reshape(-1, BLK, head_dim)
    global_ids = block_list[:, 0, :]
    shard_id = global_ids // shard_blocks
    local_index = shard_id // slab_count * shard_blocks + global_ids % shard_blocks
    counts_all = block_count[:, 0]
    query_blocks = query_all.shape[0] // BLK
    group_size = 8
    groups = query_blocks // group_size

    def attend(items):
        query_group, tangent_group, picked, counts = items
        flat = picked.reshape(-1)
        key_rows = key_blocks[flat].reshape(group_size, -1, head_dim)
        value_rows = value_blocks[flat].reshape(group_size, -1, head_dim)
        keyt_rows = keyt_blocks[flat].reshape(group_size, -1, head_dim)
        valuet_rows = valuet_blocks[flat].reshape(group_size, -1, head_dim)
        active = jnp.repeat(jnp.arange(LMAX)[None, :] < counts[:, None], BLK, axis=1)
        scores = (
            jnp.einsum("gqd,gkd->gqk", query_group, key_rows, preferred_element_type=jnp.float32)
            * score_scale
        )
        score_tangent = (
            jnp.einsum("gqd,gkd->gqk", tangent_group, key_rows, preferred_element_type=jnp.float32)
            + jnp.einsum("gqd,gkd->gqk", query_group, keyt_rows, preferred_element_type=jnp.float32)
        ) * score_scale
        peak = jnp.max(jnp.where(active[:, None, :], scores, -jnp.inf), axis=2)
        weights = jnp.where(active[:, None, :], jnp.exp(scores - peak[:, :, None]), 0.0)
        total = jnp.sum(weights, axis=2)
        slope = jnp.sum(weights * score_tangent, axis=2)
        weights_b = weights.astype(jnp.bfloat16)
        scaled_b = (weights * score_tangent).astype(jnp.bfloat16)
        weighted = jnp.einsum(
            "gqk,gkd->gqd", weights_b, value_rows, preferred_element_type=jnp.float32
        )
        tangent_sum = jnp.einsum(
            "gqk,gkd->gqd", scaled_b, value_rows, preferred_element_type=jnp.float32
        ) + jnp.einsum("gqk,gkd->gqd", weights_b, valuet_rows, preferred_element_type=jnp.float32)
        return (peak, total, weighted, slope, tangent_sum)

    peak, total, weighted, slope, tangent_sum = lax.map(
        attend,
        (
            query_all.reshape(groups, group_size, BLK, head_dim),
            qtangent_all.reshape(groups, group_size, BLK, head_dim),
            local_index.reshape(groups, group_size, LMAX),
            counts_all.reshape(groups, group_size),
        ),
    )
    slab_rows = query_all.shape[0]
    peak = peak.reshape(slab_rows)
    total = total.reshape(slab_rows)
    slope = slope.reshape(slab_rows)
    weighted = weighted.reshape(slab_rows, head_dim)
    tangent_sum = tangent_sum.reshape(slab_rows, head_dim)
    peak_all = lax.pmax(peak, "kv")
    factor = jnp.exp(peak - peak_all)
    total_own, weighted_own, slope_own, tangent_own = (
        lax.psum_scatter(total * factor, "kv", scatter_dimension=0, tiled=True),
        lax.psum_scatter(weighted * factor[:, None], "kv", scatter_dimension=0, tiled=True),
        lax.psum_scatter(slope * factor, "kv", scatter_dimension=0, tiled=True),
        lax.psum_scatter(tangent_sum * factor[:, None], "kv", scatter_dimension=0, tiled=True),
    )
    output = weighted_own / total_own[:, None]
    output_tangent = tangent_own / total_own[:, None] - (slope_own / total_own)[:, None] * output
    return (output.astype(jnp.bfloat16), output_tangent.astype(jnp.bfloat16))


def solution(mesh):
    in_specs = (
        P(("pb", "kv"), None),
        P(("pb", "kv"), None),
        P(("pb", "kv"), None),
        P(("pb", "kv"), None),
        P(("pb", "kv"), None),
        P(("pb", "kv"), None),
        P("pb", "kv", None),
        P("pb", "kv"),
    )
    out_specs = (P(("pb", "kv"), None), P(("pb", "kv"), None))
    return jax.shard_map(shards, mesh=mesh, in_specs=in_specs, out_specs=out_specs, check_vma=False)
```

profile of v0, /device:TPU:0, one launch (start us, length us, event | category | flops | bytes accessed | tf_op | source)
XLA Modules:
  0.0 322.6 jit_solution(14211954801585777682)
XLA Ops:
  7.2 0.0 reduce-scatter.3.cloned.1.call-start
  7.3 0.5 broadcast.93
  7.8 1.3 reduce.3
  9.1 0.1 reshape_squeeze.3
  9.2 35.4 %all_gather.18 = bf16[2048,128]{1,0:T(8,128)(2,1)} all-gather(bf16[256,128]{1,0:T(8,128)(2,1)} %param.10), channel_id=1, replica_groups=mesh['pb'=4,'kv'=8] {'kv'}, dimensions={0}, use_global_device_ids=true | all-gather | bytes 589824 | tf_op jit(solution)/shard_map/all_gather | solution.py:20
  44.6 33.6 %all_gather.21 = bf16[2048,128]{1,0:T(8,128)(2,1)} all-gather(bf16[256,128]{1,0:T(8,128)(2,1)} %param.11), channel_id=1, replica_groups=mesh['pb'=4,'kv'=8] {'kv'}, dimensions={0}, use_global_device_ids=true | all-gather | bytes 589824 | tf_op jit(solution)/shard_map/all_gather | solution.py:21
  78.2 6.0 %all_gather.19 = bf16[1024,128]{1,0:T(8,128)(2,1)S(1)} all-gather(bf16[256,128]{1,0:T(8,128)(2,1)} %param.12), channel_id=1, replica_groups=mesh['pb'=4,'kv'=8] {'pb'}, dimensions={0}, use_global_device_ids=true | all-gather | bytes 327680 | tf_op jit(solution)/shard_map/all_gather | solution.py:24
  84.2 6.0 %all_gather.20 = bf16[1024,128]{1,0:T(8,128)(2,1)S(1)} all-gather(bf16[256,128]{1,0:T(8,128)(2,1)} %param.13), channel_id=1, replica_groups=mesh['pb'=4,'kv'=8] {'pb'}, dimensions={0}, use_global_device_ids=true | all-gather | bytes 327680 | tf_op jit(solution)/shard_map/all_gather | solution.py:25
  90.2 6.0 %all_gather.22 = bf16[1024,128]{1,0:T(8,128)(2,1)S(1)} all-gather(bf16[256,128]{1,0:T(8,128)(2,1)} %param.14), channel_id=1, replica_groups=mesh['pb'=4,'kv'=8] {'pb'}, dimensions={0}, use_global_device_ids=true | all-gather | bytes 327680 | tf_op jit(solution)/shard_map/all_gather | solution.py:26
  96.3 6.0 %all_gather.23 = bf16[1024,128]{1,0:T(8,128)(2,1)S(1)} all-gather(bf16[256,128]{1,0:T(8,128)(2,1)} %param.15), channel_id=1, replica_groups=mesh['pb'=4,'kv'=8] {'pb'}, dimensions={0}, use_global_device_ids=true | all-gather | bytes 327680 | tf_op jit(solution)/shard_map/all_gather | solution.py:27
  102.3 0.8 squeeze.14
  103.1 0.1 fusion.27
  103.2 57.1 %while.18 = (s32[]{:T(128)}, f32[2,8,128]{2,1,0:T(8,128)S(1)}, f32[2,8,128]{2,1,0:T(8,128)S(1)}, f32[2,8,128,128]{3,2,1,0:T(8,128)}, f32[2,8,128]{2,1,0:T(8,128)...) while((s32[]{:T(128)}, f32[2,8,128]{2,1,0:T(8,128)S(1)}, ...), condition=%wide.region_4.5_spmd, body=%wide.region_0.4_spmd.sunk | while | flops 1634859264 | bytes 101561608 | solution.py:71
  103.2 0.1 copy.14
  103.2 0.1 reshape.163
  103.3 1.0 gather_fusion
  104.3 0.0 copy-start.2
  104.3 0.1 broadcast_bitcast_fusion.2
  104.4 3.6 %select_reduce_fusion.2 = (f32[8,128]{1,0:T(8,128)S(1)}, f32[8,128,1024]{2,1,0:T(8,128)}) fusion(pred[8,1024]{1,0:T(8,128)(4,1)S(1)} %broadcast_bitcast_fusion.2, bf16[8,1024,128]{2,1,0:T(8,128)(2,1)S(1)} %bitcast.106, bf16[2,8,128,128]{3,2,1,0:T(8,128)(2,1)} %get-tuple-element.291, s32[]{:T(128)} %get-tuple-element.269), kind=kOutput, calls=%fused_computation.6.clone.1 | convolution fusion | flops 271580160 | bytes 6566400 | tf_op jit(solution)/shard_map/while/body/eval_jaxpr/gqd,gkd->gqk/dot_general | solution.py:50
  108.1 0.0 copy-done.2
  108.1 2.7 fusion.66
  110.7 2.2 gather_fusion.1
  112.9 5.8 %fusion.67 = (f32[8,128]{1,0:T(8,128)S(1)}, bf16[8,128,1024]{2,1,0:T(8,128)(2,1)S(1)}) fusion(f32[8,128,1024]{2,1,0:T(8,128)} %fusion.66, bf16[8,1024,128]{2,1,0:T(8,128)(2,1)} %bitcast.112, bf16[2,8,128,128]{3,2,1,0:T(8,128)(2,1)} %get-tuple-element.291, s32[]{:T(128)} %get-tuple-element.269, f32[8,128]{1,0:T(8,128)S(1)} %get-tuple-element.248, ...), kind=kOutput, calls=%fused_computation.61.clone.1 | convolution fusion | flops 276823040 | bytes 12861952 | tf_op jit(solution)/shard_map/while/body/eval_jaxpr/gqd,gkd->gqk/dot_general | solution.py:55
  118.7 2.1 gather_fusion.2
  120.8 3.1 fusion.70
  123.9 0.9 gather_fusion.3
  124.9 0.0 copy-start
  124.9 0.0 copy-start.1
  124.9 0.0 copy-start.3
  124.9 4.3 %fusion.71 = f32[2,8,128,128]{3,2,1,0:T(8,128)} fusion(f32[2,8,128,128]{3,2,1,0:T(8,128)} %get-tuple-element.274, s32[]{:T(128)} %get-tuple-element.269, f32[8,128,128]{2,1,0:T(8,128)} %fusion.70, bf16[8,1024,128]{2,1,0:T(8,128)(2,1)S(1)} %bitcast.115, f32[8,128,1024]{2,1,0:T(8,128)} %get-tuple-element.249, f32[8,128]{1,0:T(8,128)S(1)} %get-tuple-element.248, ...), kind=kOutput, calls=%fused_computation.15.clone.1 | convolution fusion | flops 272760832 | bytes 7352832 | tf_op jit(solution)/shard_map/while/body/eval_jaxpr/gqk,gkd->gqd/dot_general | solution.py:68
  129.2 0.0 copy-done
  129.2 0.0 copy-done.1
  129.2 0.4 copy-done.3
  129.6 1.0 fusion.69
  130.6 0.0 copy-start.4
  130.6 1.1 fusion.68
  131.7 0.0 copy-done.4
  131.7 0.1 copy.14
  131.8 0.1 reshape.163
  131.9 1.0 gather_fusion
  132.9 0.1 broadcast_bitcast_fusion.2
  133.0 3.6 %select_reduce_fusion.2 = (f32[8,128]{1,0:T(8,128)S(1)}, f32[8,128,1024]{2,1,0:T(8,128)}) fusion(pred[8,1024]{1,0:T(8,128)(4,1)S(1)} %broadcast_bitcast_fusion.2, bf16[8,1024,128]{2,1,0:T(8,128)(2,1)S(1)} %bitcast.106, bf16[2,8,128,128]{3,2,1,0:T(8,128)(2,1)} %get-tuple-element.291, s32[]{:T(128)} %get-tuple-element.269), kind=kOutput, calls=%fused_computation.6.clone.1 | convolution fusion | flops 271580160 | bytes 6566400 | tf_op jit(solution)/shard_map/while/body/eval_jaxpr/gqd,gkd->gqk/dot_general | solution.py:50
  136.6 2.7 fusion.66
  139.3 2.2 gather_fusion.1
  141.5 5.7 %fusion.67 = (f32[8,128]{1,0:T(8,128)S(1)}, bf16[8,128,1024]{2,1,0:T(8,128)(2,1)S(1)}) fusion(f32[8,128,1024]{2,1,0:T(8,128)} %fusion.66, bf16[8,1024,128]{2,1,0:T(8,128)(2,1)} %bitcast.112, bf16[2,8,128,128]{3,2,1,0:T(8,128)(2,1)} %get-tuple-element.291, s32[]{:T(128)} %get-tuple-element.269, f32[8,128]{1,0:T(8,128)S(1)} %get-tuple-element.248, ...), kind=kOutput, calls=%fused_computation.61.clone.1 | convolution fusion | flops 276823040 | bytes 12861952 | tf_op jit(solution)/shard_map/while/body/eval_jaxpr/gqd,gkd->gqk/dot_general | solution.py:55
  147.3 2.1 gather_fusion.2
  149.4 3.1 fusion.70
  152.5 0.9 gather_fusion.3
  153.5 4.3 %fusion.71 = f32[2,8,128,128]{3,2,1,0:T(8,128)} fusion(f32[2,8,128,128]{3,2,1,0:T(8,128)} %get-tuple-element.274, s32[]{:T(128)} %get-tuple-element.269, f32[8,128,128]{2,1,0:T(8,128)} %fusion.70, bf16[8,1024,128]{2,1,0:T(8,128)(2,1)S(1)} %bitcast.115, f32[8,128,1024]{2,1,0:T(8,128)} %get-tuple-element.249, f32[8,128]{1,0:T(8,128)S(1)} %get-tuple-element.248, ...), kind=kOutput, calls=%fused_computation.15.clone.1 | convolution fusion | flops 272760832 | bytes 7352832 | tf_op jit(solution)/shard_map/while/body/eval_jaxpr/gqk,gkd->gqd/dot_general | solution.py:68
  157.8 0.4 copy-done.3
  158.1 1.0 fusion.69
  159.2 1.1 fusion.68
  160.3 0.0 copy-start.5
  160.3 21.9 %pmax.7 = f32[2048]{0:T(1024)S(1)} all-reduce(f32[2048]{0:T(1024)S(1)} %bitcast.118), channel_id=1, replica_groups=mesh['pb'=4,'kv'=8] {'kv'}, use_global_device_ids=true, to_apply=%region_5.6 | all-reduce | flops 2048 | bytes 16384 | tf_op jit(solution)/shard_map/pmax | solution.py:86
  182.3 3.2 %bitcast_multiply_fusion = (f32[2048,128]{1,0:T(8,128)}, f32[2048,128]{1,0:T(8,128)}) fusion(f32[2,8,128,128]{3,2,1,0:T(8,128)} %get-tuple-element.81, f32[2048]{0:T(1024)S(1)} %get-tuple-element.144, f32[2,8,128,128]{3,2,1,0:T(8,128)} %get-tuple-element.78), kind=kLoop, calls=%fused_computation.42 | loop fusion | flops 524288 | bytes 4202496 | tf_op jit(solution)/shard_map/mul | solution.py:92
  185.5 0.0 reduce-scatter.3.cloned.1.call-update
  185.5 0.0 reduce-scatter.5.cloned.1.call-start
  185.6 0.7 reduce-scatter.5.cloned.1.call-update
  186.3 0.6 dynamic-slice
  187.5 33.1 %all-reduce.2 = (f32[2048]{0:T(1024)S(1)}, f32[2048]{0:T(1024)S(1)}) all-reduce(f32[2048]{0:T(1024)S(1)} %bitcast_multiply_fusion.3, f32[2048]{0:T(1024)S(1)} %get-tuple-element.143), channel_id=3, replica_groups=mesh['pb'=4,'kv'=8] {'kv'}, use_global_device_ids=true, to_apply=%region_7.8.clone | all-reduce | flops 4096 | bytes 32768
  220.6 0.1 dynamic-slice_divide_fusion
  220.7 26.4 %reduce-scatter.3.cloned.1.call-done = f32[256,128]{1,0:T(8,128)} async-done(((f32[2048,128]{1,0:T(8,128)}), f32[256,128]{1,0:T(8,128)}) %reduce-scatter.3.cloned.1.call-update) | async-done | bytes 131088 | tf_op jit(solution)/shard_map/reduce_scatter | solution.py:90
  247.1 66.9 %reduce-scatter.5.cloned.1.call-done = f32[256,128]{1,0:T(8,128)} async-done(((f32[2048,128]{1,0:T(8,128)}), f32[256,128]{1,0:T(8,128)}) %reduce-scatter.5.cloned.1.call-update) | async-done | bytes 131088 | tf_op jit(solution)/shard_map/reduce_scatter | solution.py:92
  314.0 1.7 subtract_convert_fusion
  (31 shorter events, 0.2 us)
Async XLA Ops:
  7.2 239.9 %reduce-scatter.3.cloned.1.call-start = ((), (), s32[]{:S(2)}) async-start(), calls=%async_computation.2 | async-start | bytes 1179648 | tf_op jit(solution)/shard_map/reduce_scatter | solution.py:90
  104.3 3.7 %copy-start.2 = (bf16[2,8,128,128]{3,2,1,0:T(8,128)(2,1)S(1)}, bf16[2,8,128,128]{3,2,1,0:T(8,128)(2,1)}, u32[]{:S(2)}) copy-start(bf16[2,8,128,128]{3,2,1,0:T(8,128)(2,1)} %get-tuple-element.295) | copy-start | bytes 1572868 | tf_op jit(solution)/shard_map/while
  124.9 4.3 %copy-start = (f32[8,128,1024]{2,1,0:T(8,128)S(1)}, f32[8,128,1024]{2,1,0:T(8,128)}, u32[]{:S(2)}) copy-start(f32[8,128,1024]{2,1,0:T(8,128)} %get-tuple-element.249) | copy-start | bytes 12582916 | tf_op jit(solution)/shard_map/while
  124.9 4.3 %copy-start.1 = (bf16[64,128,128]{2,1,0:T(8,128)(2,1)S(1)}, bf16[64,128,128]{2,1,0:T(8,128)(2,1)}, u32[]{:S(2)}) copy-start(bf16[64,128,128]{2,1,0:T(8,128)(2,1)} %gather_fusion.2) | copy-start | bytes 6291460 | tf_op jit(solution)/shard_map/while
  124.9 4.7 %copy-start.3 = (f32[2,8,128,128]{3,2,1,0:T(8,128)S(1)}, f32[2,8,128,128]{3,2,1,0:T(8,128)}, u32[]{:S(2)}) copy-start(f32[2,8,128,128]{3,2,1,0:T(8,128)} %get-tuple-element.272) | copy-start | bytes 3145732 | tf_op jit(solution)/shard_map/while
  130.6 1.1 copy-start.4
  132.9 3.7 %copy-start.2 = (bf16[2,8,128,128]{3,2,1,0:T(8,128)(2,1)S(1)}, bf16[2,8,128,128]{3,2,1,0:T(8,128)(2,1)}, u32[]{:S(2)}) copy-start(bf16[2,8,128,128]{3,2,1,0:T(8,128)(2,1)} %get-tuple-element.295) | copy-start | bytes 1572868 | tf_op jit(solution)/shard_map/while
  153.5 4.3 %copy-start = (f32[8,128,1024]{2,1,0:T(8,128)S(1)}, f32[8,128,1024]{2,1,0:T(8,128)}, u32[]{:S(2)}) copy-start(f32[8,128,1024]{2,1,0:T(8,128)} %get-tuple-element.249) | copy-start | bytes 12582916 | tf_op jit(solution)/shard_map/while
  153.5 4.3 %copy-start.1 = (bf16[64,128,128]{2,1,0:T(8,128)(2,1)S(1)}, bf16[64,128,128]{2,1,0:T(8,128)(2,1)}, u32[]{:S(2)}) copy-start(bf16[64,128,128]{2,1,0:T(8,128)(2,1)} %gather_fusion.2) | copy-start | bytes 6291460 | tf_op jit(solution)/shard_map/while
  153.5 4.7 %copy-start.3 = (f32[2,8,128,128]{3,2,1,0:T(8,128)S(1)}, f32[2,8,128,128]{3,2,1,0:T(8,128)}, u32[]{:S(2)}) copy-start(f32[2,8,128,128]{3,2,1,0:T(8,128)} %get-tuple-element.272) | copy-start | bytes 3145732 | tf_op jit(solution)/shard_map/while
  159.1 1.1 copy-start.4
  160.3 26.0 %copy-start.5 = (u32[32]{0:T(128)S(1)}, u32[32]{0:T(128)}, u32[]{:S(2)}) copy-start(u32[32]{0:T(128)} %constant.74) | copy-start | bytes 388
  185.5 128.5 %reduce-scatter.5.cloned.1.call-start = ((), (), s32[]{:S(2)}) async-start(), calls=%async_computation.3 | async-start | bytes 1179648 | tf_op jit(solution)/shard_map/reduce_scatter | solution.py:92
Sparse Core Ops, SparseCore 0:
  185.6 61.3 reduce-scatter.2
  250.5 63.4 reduce-scatter.4
where the time goes:
time: 323 us
  blocking collectives  148 us (46%)
  waiting for transfers between devices  94 us (29%)
  matrix products  40.8 us (13%)
  local copies, waits for them, and re-layouts  15.8 us (5%)
  between operations  14.8 us (5%)
  other arithmetic  8.65 us (3%)
    reduce_scatter x1, waiting for transfers between devices, shards(): lax.psum_scatter(tangent_sum * factor[:, None], 'kv', scatter_dimension=0...  66.9 us
    all_gather x1, blocking collectives, shards(): lax.all_gather(queries, 'kv', axis=0, tiled=True)  35.4 us
    all_gather x1, blocking collectives, shards(): lax.all_gather(query_tangent, 'kv', axis=0, tiled=True)  33.6 us
    unnamed x1, blocking collectives  33.1 us
    reduce_scatter x1, waiting for transfers between devices, shards(): lax.psum_scatter(weighted * factor[:, None], 'kv', scatter_dimension=0, t...  26.4 us
    pmax x1, blocking collectives, shards(): peak_all = lax.pmax(peak, 'kv')  21.9 us
    dot_general x2, matrix products, attend(): jnp.einsum('gqd,gkd->gqk', query_group, keyt_rows, preferred_element_type...  11.5 us
    dot_general x2, matrix products, attend(): jnp.einsum('gqk,gkd->gqd', weights_b, valuet_rows, preferred_element_type...  8.55 us
  transfers between devices with their start and end apart: 2, of which 2 were waited for; matrix products, arithmetic and copies ran while one was open for 0% of the time, Pallas kernels for 0%

commit v1 on v0

--- a/solution.py
+++ b/solution.py
@@ -6,6 +6,27 @@
 
 BLK = 128
 LMAX = 8
+
+
+def joined_along(parts, dim):
+    parts = jnp.moveaxis(parts, 0, dim)
+    lengths = parts.shape
+    return parts.reshape(*lengths[:dim], lengths[dim] * lengths[dim + 1], *lengths[dim + 2 :])
+
+
+def collected_by_bits(x, axis):
+    size, position = (lax.axis_size(axis), lax.axis_index(axis))
+    blocks, apart = (x[None], 1)
+    while apart < size:
+        theirs = lax.ppermute(blocks, axis, [(i, i ^ apart) for i in range(size)])
+        low = position & apart == 0
+        blocks = jnp.concatenate([jnp.where(low, blocks, theirs), jnp.where(low, theirs, blocks)])
+        apart *= 2
+    return blocks
+
+
+def doubled_up(x, axis, dim):
+    return joined_along(collected_by_bits(x, axis), dim)
 
 
 def shards(
@@ -18,7 +39,7 @@
     score_scale = 1.0 / math.sqrt(head_dim)
     query_all, qtangent_all = (
         lax.all_gather(queries, "kv", axis=0, tiled=True),
-        lax.all_gather(query_tangent, "kv", axis=0, tiled=True),
+        doubled_up(query_tangent, "kv", 0),
     )
     key_all, value_all, ktangent_all, vtangent_all = (
         lax.all_gather(keys, "pb", axis=0, tiled=True),

time: 323 us -> 293 us (0.907)
  blocking collectives: 148 us -> 110 us
  starting transfers between devices: 0.08 us -> 7.41 us
    all_gather x1 -> x0, blocking collectives: 33.6 us -> none  [shards(): lax.all_gather(query_tangent, 'kv', axis=0, tiled=True)]
    ppermute x0 -> x3, starting transfers between devices: none -> 7.33 us  [collected_by_bits(): theirs = lax.ppermute(blocks, axis, [(i, i ^ apart) for i in range(size)])]
    pmax x1, blocking collectives: 21.9 us -> 17.7 us  [shards(): peak_all = lax.pmax(peak, 'kv')]
  transfers between devices with their start and end apart: 2 -> 5, of which waited for: 2 -> 2; matrix products, arithmetic and copies ran while one was open for 0% -> 1% of each run, Pallas kernels for 0% -> 0%
where the time goes in v1:
time: 293 us
  blocking collectives  110 us (38%)
  waiting for transfers between devices  93.1 us (32%)
  matrix products  40.8 us (14%)
  local copies, waits for them, and re-layouts  15.7 us (5%)
  between operations  14.8 us (5%)
  other arithmetic  10.5 us (4%)
  starting transfers between devices  7.41 us (3%)
    reduce_scatter x1, waiting for transfers between devices, shards(): lax.psum_scatter(tangent_sum * factor[:, None], 'kv', scatter_dimension=0...  66.5 us
    unnamed x1, blocking collectives  34.9 us
    all_gather x1, blocking collectives, shards(): lax.all_gather(queries, 'kv', axis=0, tiled=True)  33.6 us
    reduce_scatter x1, waiting for transfers between devices, shards(): lax.psum_scatter(weighted * factor[:, None], 'kv', scatter_dimension=0, t...  25.9 us
    pmax x1, blocking collectives, shards(): peak_all = lax.pmax(peak, 'kv')  17.7 us
    dot_general x2, matrix products, attend(): jnp.einsum('gqd,gkd->gqk', query_group, keyt_rows, preferred_element_type...  11.5 us
    dot_general x2, matrix products, attend(): jnp.einsum('gqk,gkd->gqd', weights_b, valuet_rows, preferred_element_type...  8.52 us
    ppermute x3, starting transfers between devices, collected_by_bits(): theirs = lax.ppermute(blocks, axis, [(i, i ^ apart) for i in range(size)])  7.33 us
  transfers between devices with their start and end apart: 5, of which 2 were waited for; matrix products, arithmetic and copies ran while one was open for 1% of the time, Pallas kernels for 0%

profile of v1, /device:TPU:0, one launch (start us, length us, event | category | flops | bytes accessed | tf_op | source)
XLA Modules:
  0.0 292.7 jit_solution(5344976120434100693)
XLA Ops:
  7.2 0.0 reduce-scatter.3.cloned.1.call-start
  7.2 3.0 %collective-permute-start = (bf16[1,256,128]{2,1,0:T(8,128)(2,1)}, bf16[1,256,128]{2,1,0:T(8,128)(2,1)S(1)}, u32[]{:S(2)}, u32[]{:S(2)}) collective-permute-start(bf16[1,256,128]{2,1,0:T(8,128)(2,1)} %bitcast.121), channel_id=1, source_target_pairs={{0,1},{1,0},{2,3},{3,2},{4,5},{5,4},{6,7},{7,6},{8,9},{9,8},{10,11... | collective-permute-start | bytes 196616 | tf_op jit(solution)/shard_map/ppermute | solution.py:21
  10.2 0.8 squeeze.14
  11.0 0.1 fusion.27
  11.1 6.0 %all_gather.16 = bf16[1024,128]{1,0:T(8,128)(2,1)S(1)} all-gather(bf16[256,128]{1,0:T(8,128)(2,1)} %param.12), channel_id=1, replica_groups=mesh['pb'=4,'kv'=8] {'pb'}, dimensions={0}, use_global_device_ids=true | all-gather | bytes 327680 | tf_op jit(solution)/shard_map/all_gather | solution.py:45
  17.1 0.0 collective-permute-done
  17.1 0.9 broadcast_select_fusion.5
  17.9 1.6 collective-permute-start.1
  19.6 6.0 %all_gather.17 = bf16[1024,128]{1,0:T(8,128)(2,1)S(1)} all-gather(bf16[256,128]{1,0:T(8,128)(2,1)} %param.13), channel_id=1, replica_groups=mesh['pb'=4,'kv'=8] {'pb'}, dimensions={0}, use_global_device_ids=true | all-gather | bytes 327680 | tf_op jit(solution)/shard_map/all_gather | solution.py:46
  25.6 6.0 %all_gather.18 = bf16[1024,128]{1,0:T(8,128)(2,1)S(1)} all-gather(bf16[256,128]{1,0:T(8,128)(2,1)} %param.14), channel_id=1, replica_groups=mesh['pb'=4,'kv'=8] {'pb'}, dimensions={0}, use_global_device_ids=true | all-gather | bytes 327680 | tf_op jit(solution)/shard_map/all_gather | solution.py:47
  31.6 0.0 collective-permute-done.1
  31.7 2.7 collective-permute-start.2
  34.3 6.0 %all_gather.19 = bf16[1024,128]{1,0:T(8,128)(2,1)S(1)} all-gather(bf16[256,128]{1,0:T(8,128)(2,1)} %param.15), channel_id=1, replica_groups=mesh['pb'=4,'kv'=8] {'pb'}, dimensions={0}, use_global_device_ids=true | all-gather | bytes 327680 | tf_op jit(solution)/shard_map/all_gather | solution.py:48
  40.3 0.5 broadcast.97
  40.8 1.3 reduce.3
  42.1 0.1 reshape_squeeze.3
  42.2 33.6 %all_gather.15 = bf16[2048,128]{1,0:T(8,128)(2,1)} all-gather(bf16[256,128]{1,0:T(8,128)(2,1)} %param.10), channel_id=1, replica_groups=mesh['pb'=4,'kv'=8] {'kv'}, dimensions={0}, use_global_device_ids=true | all-gather | bytes 589824 | tf_op jit(solution)/shard_map/all_gather | solution.py:41
  75.8 0.0 collective-permute-done.2
  75.9 0.9 pad_maximum_fusion
  76.8 57.0 %while.18 = (s32[]{:T(128)}, f32[2,8,128]{2,1,0:T(8,128)S(1)}, f32[2,8,128]{2,1,0:T(8,128)S(1)}, f32[2,8,128,128]{3,2,1,0:T(8,128)}, f32[2,8,128]{2,1,0:T(8,128)...) while((s32[]{:T(128)}, f32[2,8,128]{2,1,0:T(8,128)S(1)}, ...), condition=%wide.region_4.5_spmd, body=%wide.region_0.4_spmd.sunk | while | flops 1634859264 | bytes 101561608 | solution.py:92
  76.8 0.1 copy.14
  76.9 0.1 reshape.159
  77.0 1.0 gather_fusion
  77.9 0.0 copy-start.2
  78.0 0.1 broadcast_bitcast_fusion.2
  78.0 3.6 %select_reduce_fusion.2 = (f32[8,128]{1,0:T(8,128)S(1)}, f32[8,128,1024]{2,1,0:T(8,128)}) fusion(pred[8,1024]{1,0:T(8,128)(4,1)S(1)} %broadcast_bitcast_fusion.2, bf16[8,1024,128]{2,1,0:T(8,128)(2,1)S(1)} %bitcast.109, bf16[2,8,128,128]{3,2,1,0:T(8,128)(2,1)} %get-tuple-element.297, s32[]{:T(128)} %get-tuple-element.275), kind=kOutput, calls=%fused_computation.6.clone.1 | convolution fusion | flops 271580160 | bytes 6566400 | tf_op jit(solution)/shard_map/while/body/eval_jaxpr/gqd,gkd->gqk/dot_general | solution.py:71
  81.7 2.7 fusion.66
  84.4 2.2 gather_fusion.1
  86.5 5.7 %fusion.67 = (f32[8,128]{1,0:T(8,128)S(1)}, bf16[8,128,1024]{2,1,0:T(8,128)(2,1)S(1)}) fusion(f32[8,128,1024]{2,1,0:T(8,128)} %fusion.66, bf16[8,1024,128]{2,1,0:T(8,128)(2,1)} %bitcast.115, bf16[2,8,128,128]{3,2,1,0:T(8,128)(2,1)} %get-tuple-element.297, s32[]{:T(128)} %get-tuple-element.275, f32[8,128]{1,0:T(8,128)S(1)} %get-tuple-element.254, ...), kind=kOutput, calls=%fused_computation.70.clone.1 | convolution fusion | flops 276823040 | bytes 12861952 | tf_op jit(solution)/shard_map/while/body/eval_jaxpr/gqd,gkd->gqk/dot_general | solution.py:76
  92.3 2.1 gather_fusion.2
  94.4 3.1 %fusion.70 = f32[8,128,128]{2,1,0:T(8,128)} fusion(bf16[8,1024,128]{2,1,0:T(8,128)(2,1)} %bitcast.116, bf16[8,128,1024]{2,1,0:T(8,128)(2,1)S(1)} %get-tuple-element.259), kind=kOutput, calls=%fused_computation.9.clone.1 | convolution fusion | flops 268435456 | bytes 4718592 | tf_op jit(solution)/shard_map/while/body/eval_jaxpr/gqk,gkd->gqd/dot_general | solution.py:87
  97.5 0.9 gather_fusion.3
  98.5 4.3 %fusion.71 = f32[2,8,128,128]{3,2,1,0:T(8,128)} fusion(f32[2,8,128,128]{3,2,1,0:T(8,128)} %get-tuple-element.280, s32[]{:T(128)} %get-tuple-element.275, f32[8,128,128]{2,1,0:T(8,128)} %fusion.70, bf16[8,1024,128]{2,1,0:T(8,128)(2,1)S(1)} %bitcast.118, f32[8,128,1024]{2,1,0:T(8,128)} %get-tuple-element.255, f32[8,128]{1,0:T(8,128)S(1)} %get-tuple-element.254, ...), kind=kOutput, calls=%fused_computation.15.clone.1 | convolution fusion | flops 272760832 | bytes 7352832 | tf_op jit(solution)/shard_map/while/body/eval_jaxpr/gqk,gkd->gqd/dot_general | solution.py:89
  102.7 0.0 copy-done
  102.7 0.4 copy-done.3
  103.1 1.0 fusion.69
  104.1 1.1 fusion.68
  105.3 0.1 copy.14
  105.4 0.1 reshape.159
  105.5 1.0 gather_fusion
  106.5 0.1 broadcast_bitcast_fusion.2
  106.5 3.6 %select_reduce_fusion.2 = (f32[8,128]{1,0:T(8,128)S(1)}, f32[8,128,1024]{2,1,0:T(8,128)}) fusion(pred[8,1024]{1,0:T(8,128)(4,1)S(1)} %broadcast_bitcast_fusion.2, bf16[8,1024,128]{2,1,0:T(8,128)(2,1)S(1)} %bitcast.109, bf16[2,8,128,128]{3,2,1,0:T(8,128)(2,1)} %get-tuple-element.297, s32[]{:T(128)} %get-tuple-element.275), kind=kOutput, calls=%fused_computation.6.clone.1 | convolution fusion | flops 271580160 | bytes 6566400 | tf_op jit(solution)/shard_map/while/body/eval_jaxpr/gqd,gkd->gqk/dot_general | solution.py:71
  110.2 2.7 fusion.66
  112.9 2.2 gather_fusion.1
  115.0 5.7 %fusion.67 = (f32[8,128]{1,0:T(8,128)S(1)}, bf16[8,128,1024]{2,1,0:T(8,128)(2,1)S(1)}) fusion(f32[8,128,1024]{2,1,0:T(8,128)} %fusion.66, bf16[8,1024,128]{2,1,0:T(8,128)(2,1)} %bitcast.115, bf16[2,8,128,128]{3,2,1,0:T(8,128)(2,1)} %get-tuple-element.297, s32[]{:T(128)} %get-tuple-element.275, f32[8,128]{1,0:T(8,128)S(1)} %get-tuple-element.254, ...), kind=kOutput, calls=%fused_computation.70.clone.1 | convolution fusion | flops 276823040 | bytes 12861952 | tf_op jit(solution)/shard_map/while/body/eval_jaxpr/gqd,gkd->gqk/dot_general | solution.py:76
  120.8 2.1 gather_fusion.2
  122.9 3.1 %fusion.70 = f32[8,128,128]{2,1,0:T(8,128)} fusion(bf16[8,1024,128]{2,1,0:T(8,128)(2,1)} %bitcast.116, bf16[8,128,1024]{2,1,0:T(8,128)(2,1)S(1)} %get-tuple-element.259), kind=kOutput, calls=%fused_computation.9.clone.1 | convolution fusion | flops 268435456 | bytes 4718592 | tf_op jit(solution)/shard_map/while/body/eval_jaxpr/gqk,gkd->gqd/dot_general | solution.py:87
  126.0 0.9 gather_fusion.3
  127.0 4.3 %fusion.71 = f32[2,8,128,128]{3,2,1,0:T(8,128)} fusion(f32[2,8,128,128]{3,2,1,0:T(8,128)} %get-tuple-element.280, s32[]{:T(128)} %get-tuple-element.275, f32[8,128,128]{2,1,0:T(8,128)} %fusion.70, bf16[8,1024,128]{2,1,0:T(8,128)(2,1)S(1)} %bitcast.118, f32[8,128,1024]{2,1,0:T(8,128)} %get-tuple-element.255, f32[8,128]{1,0:T(8,128)S(1)} %get-tuple-element.254, ...), kind=kOutput, calls=%fused_computation.15.clone.1 | convolution fusion | flops 272760832 | bytes 7352832 | tf_op jit(solution)/shard_map/while/body/eval_jaxpr/gqk,gkd->gqd/dot_general | solution.py:89
  131.2 0.4 copy-done.3
  131.6 1.0 fusion.69
  132.6 1.1 fusion.68
  133.8 0.0 copy-start.5
  133.8 17.7 %pmax.7 = f32[2048]{0:T(1024)S(1)} all-reduce(f32[2048]{0:T(1024)S(1)} %bitcast.122), channel_id=1, replica_groups=mesh['pb'=4,'kv'=8] {'kv'}, use_global_device_ids=true, to_apply=%region_5.6 | all-reduce | flops 2048 | bytes 16384 | tf_op jit(solution)/shard_map/pmax | solution.py:107
  151.5 3.2 %bitcast_multiply_fusion = (f32[2048,128]{1,0:T(8,128)}, f32[2048,128]{1,0:T(8,128)}) fusion(f32[2,8,128,128]{3,2,1,0:T(8,128)} %get-tuple-element.81, f32[2048]{0:T(1024)S(1)} %get-tuple-element.144, f32[2,8,128,128]{3,2,1,0:T(8,128)} %get-tuple-element.78), kind=kLoop, calls=%fused_computation.42 | loop fusion | flops 524288 | bytes 4202496 | tf_op jit(solution)/shard_map/mul | solution.py:113
  154.7 0.0 reduce-scatter.3.cloned.1.call-update
  154.7 0.0 reduce-scatter.5.cloned.1.call-start
  154.8 0.7 reduce-scatter.5.cloned.1.call-update
  155.5 0.6 dynamic-slice
  156.7 34.9 %all-reduce.2 = (f32[2048]{0:T(1024)S(1)}, f32[2048]{0:T(1024)S(1)}) all-reduce(f32[2048]{0:T(1024)S(1)} %bitcast_multiply_fusion.3, f32[2048]{0:T(1024)S(1)} %get-tuple-element.143), channel_id=3, replica_groups=mesh['pb'=4,'kv'=8] {'kv'}, use_global_device_ids=true, to_apply=%region_7.8.clone | all-reduce | flops 4096 | bytes 32768
  191.6 0.1 dynamic-slice_divide_fusion
  191.7 25.9 %reduce-scatter.3.cloned.1.call-done = f32[256,128]{1,0:T(8,128)} async-done(((f32[2048,128]{1,0:T(8,128)}), f32[256,128]{1,0:T(8,128)}) %reduce-scatter.3.cloned.1.call-update) | async-done | bytes 131088 | tf_op jit(solution)/shard_map/reduce_scatter | solution.py:111
  217.6 66.5 %reduce-scatter.5.cloned.1.call-done = f32[256,128]{1,0:T(8,128)} async-done(((f32[2048,128]{1,0:T(8,128)}), f32[256,128]{1,0:T(8,128)}) %reduce-scatter.5.cloned.1.call-update) | async-done | bytes 131088 | tf_op jit(solution)/shard_map/reduce_scatter | solution.py:113
  284.1 1.7 subtract_convert_fusion
  (42 shorter events, 0.3 us)
Async XLA Ops:
  7.2 210.4 %reduce-scatter.3.cloned.1.call-start = ((), (), s32[]{:S(2)}) async-start(), calls=%async_computation.2 | async-start | bytes 1179648 | tf_op jit(solution)/shard_map/reduce_scatter | solution.py:111
  7.2 9.9 %collective-permute-start = (bf16[1,256,128]{2,1,0:T(8,128)(2,1)}, bf16[1,256,128]{2,1,0:T(8,128)(2,1)S(1)}, u32[]{:S(2)}, u32[]{:S(2)}) collective-permute-start(bf16[1,256,128]{2,1,0:T(8,128)(2,1)} %bitcast.121), channel_id=1, source_target_pairs={{0,1},{1,0},{2,3},{3,2},{4,5},{5,4},{6,7},{7,6},{8,9},{9,8},{10,11... | collective-permute-start | bytes 196616 | tf_op jit(solution)/shard_map/ppermute | solution.py:21
  17.9 13.7 %collective-permute-start.1 = (bf16[2,256,128]{2,1,0:T(8,128)(2,1)S(1)}, bf16[2,256,128]{2,1,0:T(8,128)(2,1)S(1)}, u32[]{:S(2)}, u32[]{:S(2)}) collective-permute-start(bf16[2,256,128]{2,1,0:T(8,128)(2,1)S(1)} %pad_maximum_fusion.2), channel_id=1, source_target_pairs={{0,2},{1,3},{2,0},{3,1},{4,6},{5,7},{6,4},{7,5},{8,10},{9,11},{10,... | collective-permute-start | bytes 393224 | tf_op jit(solution)/shard_map/ppermute | solution.py:21
  31.7 44.2 %collective-permute-start.2 = (bf16[4,256,128]{2,1,0:T(8,128)(2,1)S(1)}, bf16[4,256,128]{2,1,0:T(8,128)(2,1)S(1)}, u32[]{:S(2)}, u32[]{:S(2)}) collective-permute-start(bf16[4,256,128]{2,1,0:T(8,128)(2,1)S(1)} %pad_maximum_fusion.1), channel_id=1, source_target_pairs={{0,4},{1,5},{2,6},{3,7},{4,0},{5,1},{6,2},{7,3},{8,12},{9,13},{10,... | collective-permute-start | bytes 786440 | tf_op jit(solution)/shard_map/ppermute | solution.py:21
  77.9 3.8 %copy-start.2 = (bf16[2,8,128,128]{3,2,1,0:T(8,128)(2,1)S(1)}, bf16[2,8,128,128]{3,2,1,0:T(8,128)(2,1)}, u32[]{:S(2)}) copy-start(bf16[2,8,128,128]{3,2,1,0:T(8,128)(2,1)} %get-tuple-element.301) | copy-start | bytes 1572868 | tf_op jit(solution)/shard_map/while
  98.4 4.3 %copy-start = (f32[8,128,1024]{2,1,0:T(8,128)S(1)}, f32[8,128,1024]{2,1,0:T(8,128)}, u32[]{:S(2)}) copy-start(f32[8,128,1024]{2,1,0:T(8,128)} %get-tuple-element.255) | copy-start | bytes 12582916 | tf_op jit(solution)/shard_map/while
  98.5 4.3 %copy-start.1 = (bf16[64,128,128]{2,1,0:T(8,128)(2,1)S(1)}, bf16[64,128,128]{2,1,0:T(8,128)(2,1)}, u32[]{:S(2)}) copy-start(bf16[64,128,128]{2,1,0:T(8,128)(2,1)} %gather_fusion.2) | copy-start | bytes 6291460 | tf_op jit(solution)/shard_map/while
  98.5 4.7 %copy-start.3 = (f32[2,8,128,128]{3,2,1,0:T(8,128)S(1)}, f32[2,8,128,128]{3,2,1,0:T(8,128)}, u32[]{:S(2)}) copy-start(f32[2,8,128,128]{3,2,1,0:T(8,128)} %get-tuple-element.278) | copy-start | bytes 3145732 | tf_op jit(solution)/shard_map/while
  104.1 1.1 copy-start.4
  106.4 3.8 %copy-start.2 = (bf16[2,8,128,128]{3,2,1,0:T(8,128)(2,1)S(1)}, bf16[2,8,128,128]{3,2,1,0:T(8,128)(2,1)}, u32[]{:S(2)}) copy-start(bf16[2,8,128,128]{3,2,1,0:T(8,128)(2,1)} %get-tuple-element.301) | copy-start | bytes 1572868 | tf_op jit(solution)/shard_map/while
  127.0 4.3 %copy-start = (f32[8,128,1024]{2,1,0:T(8,128)S(1)}, f32[8,128,1024]{2,1,0:T(8,128)}, u32[]{:S(2)}) copy-start(f32[8,128,1024]{2,1,0:T(8,128)} %get-tuple-element.255) | copy-start | bytes 12582916 | tf_op jit(solution)/shard_map/while
  127.0 4.3 %copy-start.1 = (bf16[64,128,128]{2,1,0:T(8,128)(2,1)S(1)}, bf16[64,128,128]{2,1,0:T(8,128)(2,1)}, u32[]{:S(2)}) copy-start(bf16[64,128,128]{2,1,0:T(8,128)(2,1)} %gather_fusion.2) | copy-start | bytes 6291460 | tf_op jit(solution)/shard_map/while
  127.0 4.7 %copy-start.3 = (f32[2,8,128,128]{3,2,1,0:T(8,128)S(1)}, f32[2,8,128,128]{3,2,1,0:T(8,128)}, u32[]{:S(2)}) copy-start(f32[2,8,128,128]{3,2,1,0:T(8,128)} %get-tuple-element.278) | copy-start | bytes 3145732 | tf_op jit(solution)/shard_map/while
  132.6 1.1 copy-start.4
  133.8 21.7 %copy-start.5 = (u32[32]{0:T(128)S(1)}, u32[32]{0:T(128)}, u32[]{:S(2)}) copy-start(u32[32]{0:T(128)} %constant.81) | copy-start | bytes 388
  154.7 129.4 %reduce-scatter.5.cloned.1.call-start = ((), (), s32[]{:S(2)}) async-start(), calls=%async_computation.3 | async-start | bytes 1179648 | tf_op jit(solution)/shard_map/reduce_scatter | solution.py:113
Sparse Core Ops, SparseCore 0:
  154.8 62.6 reduce-scatter.2
  221.0 63.0 reduce-scatter.4
